TPU v7x, 512 devices: a whole 4x4x16 slice. The times are simulated.
512 devices in a mesh: tile: 32 (over y, z_lo, core), chan: 16 (over x, z_hi).
Axes of the slice: x: 4, y: 4, z: 16 (z_hi: 4, z_lo: 4; z = z_hi * 4 + z_lo), core: 2. Of those that a mesh axis runs over, the one named last changes fastest.
Arguments:
- features: bfloat16 [256, 1536, 128], P('tile', 'chan'), may hold values from -8 to 8
- dw_weight: float32 [1536, 49], P('chan'), may hold values from -2.5 to 2.5
- dw_bias: float32 [1536], P('chan'), may hold values from -3 to 3
- ln_gain: float32 [1536], replicated, may hold values from 0.5 to 1.5
- ln_bias: float32 [1536], replicated, may hold values from -2 to 2
- w_in: bfloat16 [1536, 6144], P('tile', 'chan'), may hold values from -0.15625 to 0.15625
- b_in: float32 [6144], P('chan'), may hold values from -3 to 3
- w_out: bfloat16 [6144, 1536], P('chan', 'tile'), may hold values from -0.15625 to 0.15625
- b_out: float32 [1536], P('chan'), may hold values from -3 to 3
- gamma: float32 [1536], P('chan'), may hold values from 0.5 to 2
Outputs:
- block_out: bfloat16 [256, 1536, 128], P('tile', 'chan')
All inputs are finite; a program needn't handle non-finite values.
Results may differ from a plain program's by a relative error of at most 0.015.
Values may be sent and summed in bfloat16 or wider, within the bound.
A program may use at most 64 MiB of HBM per device.

v0:
```python
import jax
import jax.numpy as jnp
from jax import lax
from jax.sharding import PartitionSpec as P


def extended(block, sides, width):
    for axis, dim in sides:
        count = lax.axis_size(axis)
        forward = [(i, i + 1) for i in range(count - 1)]
        backward = [(target, source) for source, target in forward]
        low = lax.ppermute(
            lax.slice_in_dim(block, block.shape[dim] - width, None, axis=dim), axis, forward
        )
        high = lax.ppermute(lax.slice_in_dim(block, 0, width, axis=dim), axis, backward)
        block = jnp.concatenate([low, block, high], axis=dim)
    return block


def local(features, dw_weight, dw_bias, ln_gain, ln_bias, w_in, b_in, w_out, b_out, gamma):
    row_count, slab_width, column_count = features.shape
    chan_count = lax.axis_size("chan")
    total_channels = slab_width * chan_count
    with_rims = extended(features, (("tile", 0),), 3)
    padded = jnp.pad(with_rims.astype(jnp.float32), ((0, 0), (0, 0), (3, 3)))
    convolved = (
        jnp.zeros((row_count, slab_width, column_count), jnp.float32) + dw_bias[None, :, None]
    )
    kernel_side = 7
    for tap_row in range(kernel_side):
        for tap_col in range(kernel_side):
            window = padded[tap_row : tap_row + row_count, :, tap_col : tap_col + column_count]
            convolved = (
                convolved + window * dw_weight[:, tap_row * kernel_side + tap_col][None, :, None]
            )
    conv_out = convolved.astype(jnp.bfloat16)
    values = conv_out.astype(jnp.float32)
    offset = lax.axis_index("chan") * slab_width
    gain_slab = lax.dynamic_slice_in_dim(ln_gain, offset, slab_width)
    shift_slab = lax.dynamic_slice_in_dim(ln_bias, offset, slab_width)
    channel_total = lax.psum(jnp.sum(values, axis=1), "chan")
    centered = values - (channel_total / total_channels)[:, None, :]
    square_total = lax.psum(jnp.sum(centered * centered, axis=1), "chan")
    variance = (square_total / total_channels)[:, None, :]
    normed_slab = (
        centered * lax.rsqrt(variance + 1e-06) * gain_slab[None, :, None]
        + shift_slab[None, :, None]
    ).astype(jnp.bfloat16)
    gathered = lax.all_gather(normed_slab, "chan", axis=1, tiled=True)
    pre_act = jnp.einsum(
        "rcw,cf->rwf",
        gathered,
        lax.all_gather(w_in, "tile", axis=0, tiled=True),
        preferred_element_type=jnp.float32,
    )
    hidden = jax.nn.gelu(pre_act + b_in[None, None, :], approximate=False).astype(jnp.bfloat16)
    partial_out = jnp.einsum(
        "rwf,fc->rwc",
        hidden,
        lax.all_gather(w_out, "tile", axis=1, tiled=True),
        preferred_element_type=jnp.float32,
    )
    summed = lax.psum_scatter(
        partial_out.astype(jnp.bfloat16), "chan", scatter_dimension=2, tiled=True
    ).astype(jnp.float32)
    projected = jnp.transpose(summed + b_out[None, None, :], (0, 2, 1))
    return (features.astype(jnp.float32) + gamma[None, :, None] * projected).astype(jnp.bfloat16)


def solution(mesh):
    placed = (
        P("tile", "chan", None),
        P("chan", None),
        P("chan"),
        P(),
        P(),
        P("tile", "chan"),
        P("chan"),
        P("chan", "tile"),
        P("chan"),
        P("chan"),
    )
    return jax.shard_map(
        local, mesh=mesh, in_specs=placed, out_specs=P("tile", "chan", None), check_vma=False
    )
```

profile of v0, /device:TPU:6, one launch (start us, length us, event | category | flops | bytes accessed | tf_op | source)
XLA Modules:
  0.0 461.6 jit_solution(4218733012855698152)
XLA Ops:
  6.5 0.7 all-gather.6.cloned.1.call-update
  7.3 0.0 all-gather.4.cloned.1.call-start
  7.3 0.9 fusion.180
  8.2 1.7 collective-permute-start
  10.0 1.3 collective-permute-start.1
  11.3 1.0 slice_bitcast_fusion.48
  12.3 1.0 slice_bitcast_fusion.47
  13.3 0.9 slice_bitcast_fusion.46
  14.2 0.8 dynamic_slice.6
  15.0 0.8 dynamic_slice.7
  15.8 0.0 collective-permute-done
  15.8 0.0 collective-permute-done.1
  15.8 1.0 maximum_convert_fusion
  16.8 0.0 copy-start.3
  16.8 6.0 %convert_reduce_fusion = (f32[8,128]{1,0:T(8,128)S(1)}, bf16[8,96,128]{2,1,0:T(8,128)(2,1)S(1)}) fusion(f32[96]{0:T(128)S(1)} %get-tuple-element.58, f32[96]{0:T(128)S(1)} %get-tuple-element.59, f32[96]{0:T(128)S(1)} %get-tuple-element.12, f32[96]{0:T(128)S(1)} %get-tuple-element.13, f32[14,96,128]{2,1,0:T(8,128)S(1)} %maximum_convert_fusion, ...), kind=kLoop, calls=%fused_computation.101 | loop fusion | flops 9927680 | bytes 3666816 | tf_op jit(solution)/shard_map/reduce_sum | solution.py:41
  22.8 53.9 %psum.14 = f32[8,128]{1,0:T(8,128)S(1)} all-reduce(f32[8,128]{1,0:T(8,128)S(1)} %get-tuple-element.7), channel_id=1, replica_groups=mesh['tile'=32,'chan'=16] {'chan'}, use_global_device_ids=true, to_apply=%region_1.2 | all-reduce | flops 1024 | bytes 8192 | tf_op jit(solution)/shard_map/psum | solution.py:41
  76.7 0.1 fusion.47
  76.8 47.7 %psum.15 = f32[8,128]{1,0:T(8,128)S(1)} all-reduce(f32[8,128]{1,0:T(8,128)S(1)} %fusion.47), channel_id=1, replica_groups=mesh['tile'=32,'chan'=16] {'chan'}, use_global_device_ids=true, to_apply=%region_3.4 | all-reduce | flops 1024 | bytes 8192 | tf_op jit(solution)/shard_map/psum | solution.py:43
  124.5 0.8 fusion.50
  125.4 0.0 all-gather.4.cloned.1.call-update
  125.4 0.0 all-gather.8.cloned.1.call-start
  125.4 0.7 all-gather.8.cloned.1.call-update
  126.1 0.0 reduce-scatter.2.cloned.1.call-start
  126.2 0.0 all-gather.6.cloned.1.call-done
  126.2 117.4 %all-gather.4.cloned.1.call-done = bf16[8,1536,128]{2,1,0:T(8,128)(2,1)} async-done(((bf16[8,96,128]{2,1,0:T(8,128)(2,1)}), bf16[8,1536,128]{2,1,0:T(8,128)(2,1)}) %all-gather.4.cloned.1.call-update) | async-done | bytes 3145744 | tf_op jit(solution)/shard_map/all_gather | solution.py:49
  243.5 0.0 copy-done.3
  243.6 4.4 fusion.144
  247.9 57.8 %all-gather.8.cloned.1.call-done = bf16[384,1536]{0,1:T(8,128)(2,1)} async-done(((bf16[384,48]{0,1:T(8,128)(2,1)}), bf16[384,1536]{0,1:T(8,128)(2,1)}) %all-gather.8.cloned.1.call-update) | async-done | bytes 1179664 | tf_op jit(solution)/shard_map/all_gather | solution.py:60
  305.7 7.2 %convolution_convert_fusion = bf16[8,128,1536]{1,2,0:T(8,128)(2,1)} fusion(bf16[384,1536]{0,1:T(8,128)(2,1)} %all-gather.8.cloned.1.call-done, f32[8,128,384]{2,1,0:T(8,128)S(1)} %get-tuple-element.60, f32[384]{0:T(512)S(1)} %copy-done.3, u8[128,384]{1,0:T(8,128)(4,1)S(1)} %get-tuple-element.6, u8[128,384]{1,0:T(8,128)(4,1)S(1)} %get-tuple-element.5), kind=kOutput, calls=%fused_computation.42 | convolution fusion | flops 1237450752 | bytes 5998080 | tf_op jit(solution)/shard_map/rwf,fc->rwc/dot_general | solution.py:57
  313.0 0.0 reduce-scatter.2.cloned.1.call-update
  313.0 140.2 %reduce-scatter.2.cloned.1.call-done = bf16[8,128,96]{1,2,0:T(8,128)(2,1)} async-done(((bf16[8,128,1536]{1,2,0:T(8,128)(2,1)}), bf16[8,128,96]{1,2,0:T(8,128)(2,1)}) %reduce-scatter.2.cloned.1.call-update) | async-done | bytes 196624 | tf_op jit(solution)/shard_map/reduce_scatter | solution.py:63
  453.2 1.8 fusion.142
  (9 shorter events, 0.0 us)
Async XLA Ops:
  6.5 119.7 %all-gather.6.cloned.1.call-start = ((), (), s32[]{:S(2)}) async-start(), calls=%async_computation.2 | async-start | bytes 1216512 | tf_op jit(solution)/shard_map/all_gather | solution.py:53
  7.3 236.3 %all-gather.4.cloned.1.call-start = ((), (), s32[]{:S(2)}) async-start(), calls=%async_computation.1 | async-start | bytes 3342336 | tf_op jit(solution)/shard_map/all_gather | solution.py:49
  8.2 7.5 %collective-permute-start = (bf16[3,96,128]{2,1,0:T(8,128)(2,1)S(1)}, bf16[3,96,128]{2,1,0:T(8,128)(2,1)S(1)}, u32[]{:S(2)}, u32[]{:S(2)}) collective-permute-start(bf16[3,96,128]{2,1,0:T(8,128)(2,1)S(1)} %get-tuple-element.9), channel_id=1, source_target_pairs={{0,16},{16,32},{32,48},{48,64},{64,80},{80,96},{96,112},{112,128},... | collective-permute-start | bytes 221192 | tf_op jit(solution)/shard_map/ppermute | solution.py:12
  10.0 5.8 %collective-permute-start.1 = (bf16[3,96,128]{2,1,0:T(8,128)(2,1)S(1)}, bf16[3,96,128]{2,1,0:T(8,128)(2,1)S(1)}, u32[]{:S(2)}, u32[]{:S(2)}) collective-permute-start(bf16[3,96,128]{2,1,0:T(8,128)(2,1)S(1)} %get-tuple-element.10), channel_id=1, source_target_pairs={{16,0},{32,16},{48,32},{64,48},{80,64},{96,80},{112,96},{128,112},... | collective-permute-start | bytes 221192 | tf_op jit(solution)/shard_map/ppermute | solution.py:15
  16.8 226.8 %copy-start.3 = (f32[384]{0:T(512)S(1)}, f32[384]{0:T(512)}, u32[]{:S(2)}) copy-start(f32[384]{0:T(512)} %param.16) | copy-start | bytes 4612
  125.4 180.4 %all-gather.8.cloned.1.call-start = ((), (), s32[]{:S(2)}) async-start(), calls=%async_computation.3 | async-start | bytes 1216512 | tf_op jit(solution)/shard_map/all_gather | solution.py:60
  126.1 327.1 %reduce-scatter.2.cloned.1.call-start = ((), (), s32[]{:S(2)}) async-start(), calls=%async_computation.4 | async-start | bytes 3342336 | tf_op jit(solution)/shard_map/reduce_scatter | solution.py:63
  313.0 140.2 %copy-start = (bf16[8,96,128]{2,1,0:T(8,128)(2,1)S(1)}, bf16[8,96,128]{2,1,0:T(8,128)(2,1)}, u32[]{:S(2)}) copy-start(bf16[8,96,128]{2,1,0:T(8,128)(2,1)} %param.10) | copy-start | bytes 589828
  313.0 140.2 %copy-start.1 = (f32[96]{0:T(128)S(1)}, f32[96]{0:T(128)}, u32[]{:S(2)}) copy-start(f32[96]{0:T(128)} %param.18) | copy-start | bytes 1156
  313.0 140.2 %copy-start.2 = (f32[96]{0:T(128)S(1)}, f32[96]{0:T(128)}, u32[]{:S(2)}) copy-start(f32[96]{0:T(128)} %param.19) | copy-start | bytes 1156
Sparse Core Ops, SparseCore 0:
  9.5 68.8 all-gather.5
  125.5 117.9 all-gather.3
  245.7 59.9 all-gather.7
  313.1 140.0 reduce-scatter.1
where the time goes:
time: 463 us; the launch traced here: 462 us
  waiting for transfers between devices  317 us (68%)
  blocking collectives  102 us (22%)
  between operations  13.2 us (3%)
  matrix products  11.6 us (3%)
  other arithmetic  9.73 us (2%)
  local copies, waits for them, and re-layouts  5.41 us (1%)
    reduce_scatter x1, waiting for transfers between devices, local(): lax.psum_scatter(partial_out.astype(jnp.bfloat16), 'chan', scatter_dimens...  140 us
    all_gather x1, waiting for transfers between devices, local(): gathered = lax.all_gather(normed_slab, 'chan', axis=1, tiled=True)  117 us
    all_gather x1, waiting for transfers between devices, local(): lax.all_gather(w_out, 'tile', axis=1, tiled=True)  57.8 us
    psum x1, blocking collectives, local(): channel_total = lax.psum(jnp.sum(values, axis=1), 'chan')  53.9 us
    psum x1, blocking collectives, local(): square_total = lax.psum(jnp.sum(centered * centered, axis=1), 'chan')  47.7 us
  transfers between devices with their start and end apart: 6, of which 3 were waited for; matrix products, arithmetic and copies ran while one was open for 4% of the time, Pallas kernels for 0%

commit v1 on v0

v1 whole, which is shorter than its diff:
```python
import functools

import jax
import jax.numpy as jnp
from jax import lax
from jax.experimental import pallas as pl
from jax.experimental.pallas import tpu as pltpu
from jax.sharding import PartitionSpec as P

MESH = pl.DeviceIdType.MESH
F32 = jnp.float32
BF16 = jnp.bfloat16

SLAB = 96
COLS = 384
TALL = 48
BIAS, OUT_BIAS, SCALE = 49, 50, 51

ERF_NUM = (
    0.00022905065861350646,
    0.0034082910107109506,
    0.050955695062380861,
    0.18520832239976145,
    1.128379143519084,
)
ERF_DEN = (
    -1.1791602954361697e-7,
    0.000023547966471313185,
    0.0010179625278914885,
    0.014070470171167667,
    0.11098505178285362,
    0.49746925110067538,
    1.0,
)


def poly(x, coefficients):
    total = jnp.full_like(x, coefficients[0])
    for coefficient in coefficients[1:]:
        total = total * x + coefficient
    return total


def gelu(v):
    u = jnp.clip(v * 0.7071067811865476, -3.832506856900711, 3.832506856900711)
    square = u * u
    erf = u * poly(square, ERF_NUM) / poly(square, ERF_DEN)
    return 0.5 * v * (1.0 + erf)


def body(
    f_ref, table_ref, gain_ref, shift_ref, w_in_ref, b_in_ref, w_out_ref, o_ref,
    ext, cv, xg, xt, hid, ob, rb, pz, fin, W, own_b, bb,
    halo_s, halo_r, za_s, za_r, b_s, b_r, xa_s, xa_r, rs_s, rs_r, fin_s, fin_r,
    zs, zr, ys, yf, yb, yq, cs, cr,
):
    t = lax.axis_index("tile")
    k = lax.axis_index("chan")
    x, zh = lax.div(k, 4), lax.rem(k, 4)
    y, zl, c = lax.div(t, 8), lax.rem(lax.div(t, 2), 4), lax.rem(t, 2)
    z = zh * 4 + zl

    def device(xx, yy, zz, cc):
        return {
            "tile": (yy * 4 + lax.rem(zz, 4)) * 2 + cc,
            "chan": xx * 4 + lax.div(zz, 4),
        }

    def ring(value, size):
        return lax.rem(value + size, size)

    def x_at(e):
        return device(ring(x + e, 4), y, z, c)

    def y_at(e):
        return device(x, ring(y + e, 4), z, c)

    def z_at(e):
        return device(x, y, ring(z + e, 16), c)

    def tile_at(e):
        return {"tile": ring(t + e, 32), "chan": k}

    other = device(x, y, z, 1 - c)

    def send(src, dst, send_sem, recv_sem, to):
        pltpu.make_async_remote_copy(
            src_ref=src, dst_ref=dst, send_sem=send_sem, recv_sem=recv_sem,
            device_id=to, device_id_type=MESH,
        ).start()

    def await_bytes(view, sem):
        pltpu.make_async_copy(view, view, sem).wait()

    barrier = pltpu.get_barrier_semaphore()
    partners = [tile_at(1), tile_at(-1), x_at(1), x_at(2), x_at(3), y_at(1), y_at(-1)]
    partners += [z_at(1), z_at(-1), z_at(4), z_at(8), z_at(-4), other]
    for partner in partners:
        pl.semaphore_signal(barrier, inc=1, device_id=partner, device_id_type=MESH)

    def slot(w, yy, zz):
        return W.at[w, lax.div(zz, 4), yy * 4 + lax.rem(zz, 4), c]

    mine = y * 4 + zl
    W[0, zh, mine, c] = w_in_ref[...]
    eye = (
        lax.broadcasted_iota(jnp.int32, (TALL, TALL), 0)
        == lax.broadcasted_iota(jnp.int32, (TALL, TALL), 1)
    )
    W[1, zh, mine, c] = lax.dot_general(
        jnp.where(eye, 1.0, 0.0).astype(BF16), w_out_ref[...],
        (((1,), (1,)), ((), ())), preferred_element_type=F32,
    ).astype(BF16)
    own_b[...] = jnp.broadcast_to(b_in_ref[...], (8, COLS))
    bb[zh] = own_b[...]
    ext[3:11] = f_ref[...]

    pl.semaphore_wait(barrier, len(partners))

    send(f_ref.at[5:8], ext.at[0:3], halo_s.at[0], halo_r.at[0], tile_at(1))
    send(f_ref.at[0:3], ext.at[11:14], halo_s.at[1], halo_r.at[1], tile_at(-1))

    reach = {(0, 1): 8, (0, -1): 7, (1, 1): 7, (1, -1): 8}

    def spread(w, off):
        zz = ring(z + off, 16)
        piece = slot(w, y, zz)
        for way in (1, -1):
            if off * way <= 0 and -off * way < reach[w, way]:
                send(piece, piece, zs.at[w, (1 - way) // 2],
                     zr.at[w, (1 - way) // 2, -off * way], z_at(way))
        onward = 1 - 2 * w
        send(piece, piece, ys.at[w, 0], yf.at[w, off % 16], y_at(onward))
        send(piece, piece, ys.at[w, 1], yb.at[w], y_at(-onward))

    def pass_on(w, off):
        onward = 1 - 2 * w
        piece = slot(w, ring(y - onward, 4), ring(z + off, 16))
        await_bytes(piece, yf.at[w, off % 16])
        send(piece, piece, ys.at[w, 2], yq.at[w], y_at(onward))

    def tick(s):
        for w in (0, 1):
            for way in (1, -1):
                if s <= reach[w, way]:
                    await_bytes(slot(w, y, ring(z - s * way, 16)), zr.at[w, (1 - way) // 2, s - 1])
                    spread(w, -s * way)
        relay(s - 1)

    def relay(s):
        for w in (0, 1):
            for way in (1, -1):
                if s == 0 and way == 1:
                    pass_on(w, 0)
                if s > 0 and s <= reach[w, way]:
                    pass_on(w, -s * way)

    for w in (0, 1):
        spread(w, 0)

    await_bytes(ext.at[0:3], halo_r.at[0])
    await_bytes(ext.at[11:14], halo_r.at[1])

    @pl.when(t == 0)
    def _():
        ext[0:3] = jnp.zeros((3, SLAB, 128), BF16)

    @pl.when(t == 31)
    def _():
        ext[11:14] = jnp.zeros((3, SLAB, 128), BF16)

    lane = lax.broadcasted_iota(jnp.int32, (1, 1, 128), 2)

    def convolve(i, carry):
        first = pl.multiple_of(lax.div(i, 2) * 16, 16)
        top = lax.rem(i, 2) * 4
        rows = ext[pl.ds(top, 10), pl.ds(first, 16), :].astype(F32)
        table = table_ref[pl.ds(first, 16), :]

        def column(j):
            return jnp.broadcast_to(table[:, j : j + 1], (16, 128))[None]

        total = jnp.broadcast_to(column(BIAS), (4, 16, 128))
        for tap_col in range(7):
            part = rows[0:4] * column(tap_col)
            for tap_row in range(1, 7):
                part = part + rows[tap_row : tap_row + 4] * column(tap_row * 7 + tap_col)
            d = tap_col - 3
            if d != 0:
                part = pltpu.roll(part, (-d) % 128, 2)
                inside = lane < 128 - d if d > 0 else lane >= -d
                part = jnp.where(inside, part, 0.0)
            total = total + part
        cv[pl.ds(top, 4), pl.ds(first, 16), :] = total.astype(BF16)
        return carry

    lax.fori_loop(0, 12, convolve, 0)

    def block(kk):
        return xg.at[:, pl.ds(pl.multiple_of(kk * SLAB, SLAB), SLAB), :]

    for r in (2, 1, 3):
        q = ring(zh + r, 4)
        to = device(x, y, q * 4 + zl, c)
        send(cv.at[pl.ds(2 * q, 2)], block(k), za_s.at[r - 1], za_r.at[r - 1], to)
        send(own_b, bb.at[zh], b_s.at[r - 1], b_r.at[r - 1], to)
    xg[:, pl.ds(pl.multiple_of(k * SLAB, SLAB), SLAB), :] = cv[pl.ds(2 * zh, 2)]

    def share(r):
        kk = x * 4 + ring(zh - r, 4)
        for e in (2, 1, 3):
            send(block(kk), block(kk), xa_s.at[e - 1, r], xa_r.at[e - 1, r], x_at(e))

    def arrived(r):
        await_bytes(block(x * 4 + ring(zh - r, 4)), za_r.at[r - 1])
        share(r)

    share(0)
    tick(1)
    tick(2)
    arrived(1)
    arrived(3)
    tick(3)
    arrived(2)
    tick(4)
    tick(5)
    tick(6)
    tick(7)
    tick(8)
    for r in range(4):
        for e in (1, 2, 3):
            await_bytes(block(ring(x - e, 4) * 4 + ring(zh - r, 4)), xa_r.at[e - 1, r])

    def load(j):
        return xg[:, pl.ds(pl.multiple_of(j * SLAB, SLAB), SLAB), :].astype(F32)

    def fold(v):
        return jnp.sum(v.reshape(2, SLAB // 8, 8, 128), axis=1)

    zero = jnp.zeros((2, 8, 128), F32)
    total = lax.fori_loop(0, 16, lambda j, s: s + fold(load(j)), zero)
    mean = jnp.sum(total, axis=1, keepdims=True) / 1536.0

    def squares(j, s):
        centered = load(j) - mean
        return s + fold(centered * centered)

    total = lax.fori_loop(0, 16, squares, zero)
    scale = lax.rsqrt(jnp.sum(total, axis=1, keepdims=True) / 1536.0 + 1e-6)

    def normalize(j, carry):
        at = pl.ds(pl.multiple_of(j * 128, 128), 128)
        for r in range(2):
            v = (xg[r, at, :].astype(F32) - mean[r]) * scale[r]
            v = v.T * gain_ref[:, at] + shift_ref[:, at]
            xt[r * 128 : r * 128 + 128, at] = v.astype(BF16)
        return carry

    lax.fori_loop(0, 12, normalize, 0)
    relay(8)

    def row(w, yy, cc):
        return W.at[w, :, pl.ds(yy * 4, 4), cc]

    def across(w, o):
        view = row(w, ring(y + o, 4), c)
        send(view, view, cs.at[w, o % 4], cr.at[w, o % 4], other)

    def collect(w):
        onward = 1 - 2 * w
        across(w, 0)
        across(w, -onward)
        await_bytes(row(w, ring(y + onward, 4), c), yb.at[w])
        across(w, onward)
        await_bytes(row(w, ring(y + 2, 4), c), yq.at[w])
        across(w, 2)

    def crossed(w, o):
        await_bytes(row(w, ring(y + o, 4), 1 - c), cr.at[w, o % 4])

    collect(0)
    for r in (1, 2, 3):
        await_bytes(bb.at[ring(zh - r, 4)], b_r.at[r - 1])
    for o in (0, -1, 1, 2):
        crossed(0, o)

    def expand(g, carry):
        pre = jnp.dot(xt[...], W[0, g].reshape(1536, COLS), preferred_element_type=F32)
        hid[g] = gelu(pre + bb[g, 0:1, :]).astype(BF16)
        return carry

    lax.fori_loop(0, 4, expand, 0)
    collect(1)

    for o in (0, 1, -1, 2):
        crossed(1, o)
        to_x = ring(y + o, 4)

        def add(g, s):
            weights = W[1, g, pl.ds(to_x * 4, 4)].reshape(COLS, COLS)
            return s + lax.dot_general(
                weights, hid[g], (((1,), (1,)), ((), ())), preferred_element_type=F32
            )

        part = lax.fori_loop(0, 4, add, jnp.zeros((COLS, 256), F32)).astype(BF16)
        ob[to_x, 0] = part[:, 0:128]
        ob[to_x, 1] = part[:, 128:256]

        @pl.when(to_x != x)
        def _():
            send(ob.at[to_x], rb.at[x], rs_s.at[to_x], rs_r.at[x], device(to_x, y, z, c))

    for e in (1, 2, 3):
        await_bytes(rb.at[ring(x + e, 4)], rs_r.at[ring(x + e, 4)])

    def reduce(i, carry):
        at = pl.ds(pl.multiple_of(i * 32, 32), 32)
        s = ob[x, :, at, :].astype(F32)
        for e in (1, 2, 3):
            s = s + rb[ring(x + e, 4), :, at, :].astype(F32)
        pz[:, at, :] = s.astype(BF16)
        return carry

    lax.fori_loop(0, 12, reduce, 0)

    for r in (2, 1, 3):
        q = ring(zh + r, 4)
        to = device(x, y, q * 4 + zl, c)
        src = pz.at[:, pl.ds(pl.multiple_of(q * SLAB, SLAB), SLAB), :]
        send(src, fin.at[pl.ds(2 * zh, 2)], fin_s.at[r - 1], fin_r.at[r - 1], to)
    fin[pl.ds(2 * zh, 2)] = pz[:, pl.ds(pl.multiple_of(zh * SLAB, SLAB), SLAB), :]
    for r in (1, 3, 2):
        await_bytes(fin.at[pl.ds(2 * ring(zh - r, 4), 2)], fin_r.at[r - 1])

    def finish(i, carry):
        at = pl.ds(pl.multiple_of(i * 16, 16), 16)
        table = table_ref[at, :]
        shift = jnp.broadcast_to(table[:, OUT_BIAS : OUT_BIAS + 1], (16, 128))[None]
        gamma = jnp.broadcast_to(table[:, SCALE : SCALE + 1], (16, 128))[None]
        projected = fin[:, at, :].astype(F32) + shift
        o_ref[:, at, :] = (f_ref[:, at, :].astype(F32) + gamma * projected).astype(BF16)
        return carry

    lax.fori_loop(0, 6, finish, 0)

    await_bytes(f_ref.at[5:8], halo_s.at[0])
    await_bytes(f_ref.at[0:3], halo_s.at[1])
    for r in range(3):
        await_bytes(cv.at[0:2], za_s.at[r])
        await_bytes(own_b, b_s.at[r])
        await_bytes(cv.at[0:2], fin_s.at[r])
        for b in range(4):
            await_bytes(cv.at[0:2], xa_s.at[r, b])
        await_bytes(ob.at[0], rs_s.at[ring(x + r + 1, 4)])
    for w in (0, 1):
        for way in (1, -1):
            count = reach[w, way]
            view = W.at[w, 0, 0:count, c]
            await_bytes(view, zs.at[w, (1 - way) // 2])
        for i in range(3):
            await_bytes(row(w, y, c), ys.at[w, i])
        for o in range(4):
            await_bytes(row(w, y, c), cs.at[w, o])


def local(features, dw_weight, dw_bias, ln_gain, ln_bias, w_in, b_in, w_out, b_out, gamma):
    table = jnp.concatenate(
        [dw_weight, dw_bias[:, None], b_out[:, None], gamma[:, None]], axis=1
    )
    dma = pltpu.SemaphoreType.DMA
    vmem = pl.BlockSpec(memory_space=pltpu.VMEM)
    return pl.pallas_call(
        body,
        out_shape=jax.ShapeDtypeStruct(features.shape, BF16),
        in_specs=[vmem] * 7,
        out_specs=vmem,
        scratch_shapes=[
            pltpu.VMEM((14, SLAB, 128), BF16),
            pltpu.VMEM((8, SLAB, 128), BF16),
            pltpu.VMEM((2, 1536, 128), BF16),
            pltpu.VMEM((256, 1536), BF16),
            pltpu.VMEM((4, 256, COLS), BF16),
            pltpu.VMEM((4, 2, COLS, 128), BF16),
            pltpu.VMEM((4, 2, COLS, 128), BF16),
            pltpu.VMEM((2, COLS, 128), BF16),
            pltpu.VMEM((8, SLAB, 128), BF16),
            pltpu.VMEM((2, 4, 16, 2, TALL, COLS), BF16),
            pltpu.VMEM((8, COLS), F32),
            pltpu.VMEM((4, 8, COLS), F32),
            dma((2,)), dma((2,)),
            dma((3,)), dma((3,)),
            dma((3,)), dma((3,)),
            dma((3, 4)), dma((3, 4)),
            dma((4,)), dma((4,)),
            dma((3,)), dma((3,)),
            dma((2, 2)), dma((2, 2, 8)),
            dma((2, 3)), dma((2, 16)), dma((2,)), dma((2,)),
            dma((2, 4)), dma((2, 4)),
        ],
        compiler_params=pltpu.CompilerParams(
            collective_id=0, has_side_effects=True, vmem_limit_bytes=48 * 2**20
        ),
        name="block",
    )(
        features, table, ln_gain[None, :], ln_bias[None, :], w_in, b_in[None, :], w_out
    )


def solution(mesh):
    placed = (
        P("tile", "chan", None),
        P("chan", None),
        P("chan"),
        P(),
        P(),
        P("tile", "chan"),
        P("chan"),
        P("chan", "tile"),
        P("chan"),
        P("chan"),
    )
    return jax.shard_map(
        local, mesh=mesh, in_specs=placed, out_specs=P("tile", "chan", None), check_vma=False
    )
```

time: 463 us -> 115 us (0.25)
  the two profiles are of different devices: /device:TPU:6 before, /device:TPU:17 now
where the time goes in v1:
time: 115 us; the launch traced here: 114 us
  Pallas kernels  109 us (95%)
  local copies, waits for them, and re-layouts  5.59 us (5%)
    pallas_call x1, Pallas kernels, local(): pl.pallas_call(body, out_shape=jax.ShapeDtypeStruct(features.shape, BF16)...  109 us
    unnamed x19, local copies, waits for them, and re-layouts  3.87 us

profile of v1, /device:TPU:17, one launch (start us, length us, event | category | flops | bytes accessed | tf_op | source)
XLA Modules:
  0.0 114.4 jit_solution(950996666583958218)
XLA Ops:
  0.0 0.0 copy-start.4
  0.0 0.0 copy-start.3
  0.0 0.7 broadcast_in_dim.23.b_in_ref
  0.7 0.0 copy-done.4
  0.7 0.7 broadcast_in_dim.22.shift_ref
  1.4 0.0 copy-done.3
  1.4 0.0 copy-start.5
  1.4 0.1 copy.11
  1.5 0.6 copy-done.5
  2.1 0.0 copy-start.6
  2.1 0.1 copy.12
  2.2 0.5 copy-done.6
  2.7 0.0 copy-start.7
  2.7 0.1 copy.13
  2.8 0.5 copy-done.7
  3.4 0.1 copy.14
  3.5 0.0 copy-start.2
  3.5 0.0 copy-start
  3.5 0.1 pad_maximum_fusion.table_ref
  3.6 0.6 copy-done.2
  4.3 0.0 copy-start.1
  4.3 0.1 copy.15.w_out_ref
  4.4 0.1 copy-done
  4.4 0.6 copy-done.1
  5.1 108.7 %block.1 = bf16[8,96,128]{2,1,0:T(8,128)(2,1)S(1)} custom-call(bf16[8,96,128]{2,1,0:T(8,128)(2,1)S(1)} %copy-done, f32[96,52]{1,0:T(8,128)S(1)} %pad_maximum_fusion.table_ref, f32[1,1536]{1,0:T(1,128)S(1)} %broadcast_in_dim.21.gain_ref, f32[1,1536]{1,0:T(1,128)S(1)} %broadcast_in_dim.22.shift_ref, bf16[48,384]{1,0:T(8,128)(2,1)S(1)} %copy-done.1, ...), custom_call_target="tpu_custom_call" | custom-call | tf_op jit(solution)/shard_map/block/pallas_call | solution.py:372
  113.8 0.7 copy.17
  (1 shorter events, 0.0 us)
Async XLA Ops:
  0.0 0.7 copy-start.4
  0.0 1.4 %copy-start.3 = (f32[96,49]{0,1:T(8,128)S(1)}, f32[96,49]{0,1:T(8,128)}, u32[]{:S(2)}) copy-start(f32[96,49]{0,1:T(8,128)} %param.11) | copy-start | bytes 56452
  1.4 0.7 copy-start.5
  2.1 0.7 copy-start.6
  2.7 0.7 copy-start.7
  3.5 0.8 copy-start.2
  3.5 0.9 copy-start
  4.3 0.8 copy-start.1

commit v2 on v1

v2 whole, which is shorter than its diff:
```python
import functools

import jax
import jax.numpy as jnp
from jax import lax
from jax.experimental import pallas as pl
from jax.experimental.pallas import tpu as pltpu
from jax.sharding import PartitionSpec as P

MESH = pl.DeviceIdType.MESH
F32 = jnp.float32
BF16 = jnp.bfloat16

SLAB = 96
COLS = 384
TALL = 48
TAPS = 49
FIRST, SECOND = 4, 6
LAG = 0
BIAS, OUT_BIAS, SCALE = 49, 50, 51

ERF_NUM = (
    0.00022905065861350646,
    0.0034082910107109506,
    0.050955695062380861,
    0.18520832239976145,
    1.128379143519084,
)
ERF_DEN = (
    -1.1791602954361697e-7,
    0.000023547966471313185,
    0.0010179625278914885,
    0.014070470171167667,
    0.11098505178285362,
    0.49746925110067538,
    1.0,
)


def poly(x, coefficients):
    total = jnp.full_like(x, coefficients[0])
    for coefficient in coefficients[1:]:
        total = total * x + coefficient
    return total


def gelu(v):
    u = jnp.clip(v * 0.7071067811865476, -3.832506856900711, 3.832506856900711)
    square = u * u
    erf = u * poly(square, ERF_NUM) / poly(square, ERF_DEN)
    return 0.5 * v * (1.0 + erf)


def body(
    f_hbm, table_hbm, dw_bias_hbm, b_out_hbm, gamma_hbm, gain_hbm, shift_hbm, w_in_hbm,
    b_in_hbm, w_out_hbm, o_ref,
    f_ref, table_ref, dw_bias_ref, b_out_ref, gamma_ref, gain_ref, shift_ref, b_in_ref,
    fetch_s, columns, planes, wide, halo, conv, cv, xg, xt, hid, ob, rb, pz, fin, W, own_b, bb,
    halo_s, halo_r, za_s, za_r, b_s, b_r, xa_s, xa_r, rs_s, rs_r, fin_s, fin_r,
    zs, zr, ys, yf, yb, yq, cs, cr,
):
    t = lax.axis_index("tile")
    k = lax.axis_index("chan")
    x, zh = lax.div(k, 4), lax.rem(k, 4)
    y, zl, c = lax.div(t, 8), lax.rem(lax.div(t, 2), 4), lax.rem(t, 2)
    z = zh * 4 + zl

    def device(xx, yy, zz, cc):
        return {
            "tile": (yy * 4 + lax.rem(zz, 4)) * 2 + cc,
            "chan": xx * 4 + lax.div(zz, 4),
        }

    def ring(value, size):
        return lax.rem(value + size, size)

    def x_at(e):
        return device(ring(x + e, 4), y, z, c)

    def y_at(e):
        return device(x, ring(y + e, 4), z, c)

    def z_at(e):
        return device(x, y, ring(z + e, 16), c)

    def tile_at(e):
        return {"tile": ring(t + e, 32), "chan": k}

    other = device(x, y, z, 1 - c)

    def send(src, dst, send_sem, recv_sem, to):
        pltpu.make_async_remote_copy(
            src_ref=src, dst_ref=dst, send_sem=send_sem, recv_sem=recv_sem,
            device_id=to, device_id_type=MESH,
        ).start()

    def await_bytes(view, sem):
        pltpu.make_async_copy(view, view, sem).wait()

    mine = y * 4 + zl
    fetches = [
        pltpu.make_async_copy(src, dst, fetch_s.at[i])
        for i, (src, dst) in enumerate((
            (w_in_hbm, W.at[0, zh, mine, c]), (w_out_hbm, W.at[1, zh, mine, c]), (f_hbm, f_ref),
            (table_hbm, table_ref), (dw_bias_hbm, dw_bias_ref), (b_out_hbm, b_out_ref),
            (gamma_hbm, gamma_ref), (gain_hbm, gain_ref), (shift_hbm, shift_ref),
            (b_in_hbm, b_in_ref),
        ))
    ]

    barrier = pltpu.get_barrier_semaphore()
    partners = [tile_at(1), tile_at(-1), x_at(1), x_at(2), x_at(3), y_at(1), y_at(-1)]
    partners += [z_at(1), z_at(-1), z_at(2), z_at(-2), z_at(6), z_at(-6), other]
    for partner in partners:
        pl.semaphore_signal(barrier, inc=1, device_id=partner, device_id_type=MESH)
    for fetch in fetches:
        fetch.start()

    def slot(w, yy, zz):
        return W.at[w, lax.div(zz, 4), yy * 4 + lax.rem(zz, 4), c]

    for fetch in fetches:
        fetch.wait()
    pl.semaphore_wait(barrier, len(partners))

    send(f_ref.at[5:8], halo.at[0], halo_s.at[0], halo_r.at[0], tile_at(1))
    send(f_ref.at[0:3], halo.at[1], halo_s.at[1], halo_r.at[1], tile_at(-1))

    reach = {(0, 1): 8, (0, -1): 7, (1, 1): 7, (1, -1): 8}

    def spread(w, off):
        zz = ring(z + off, 16)
        piece = slot(w, y, zz)
        for way in (1, -1):
            if off * way <= 0 and -off * way < reach[w, way]:
                send(piece, piece, zs.at[w, (1 - way) // 2],
                     zr.at[w, (1 - way) // 2, -off * way], z_at(way))
        onward = heading(w, off)
        send(piece, piece, ys.at[w, 0], yf.at[w, off % 16], y_at(onward))
        send(piece, piece, ys.at[w, 1], yb.at[w, off % 16], y_at(-onward))
        cross(w, 0, piece)

    def cross(w, o, piece):
        send(piece, piece, cs.at[w, o], cr.at[w, o], other)

    def heading(w, off):
        return 1 if off < 0 or (off == 0 and w == 0) else -1

    def pass_on(w, off):
        onward = heading(w, off)
        piece = slot(w, ring(y - onward, 4), ring(z + off, 16))
        await_bytes(piece, yf.at[w, off % 16])
        send(piece, piece, ys.at[w, 2], yq.at[w, off % 16], y_at(onward))
        cross(w, -onward % 4, piece)
        piece = slot(w, ring(y + onward, 4), ring(z + off, 16))
        await_bytes(piece, yb.at[w, off % 16])
        cross(w, onward % 4, piece)

    def last(w, off):
        piece = slot(w, ring(y + 2, 4), ring(z + off, 16))
        await_bytes(piece, yq.at[w, off % 16])
        cross(w, 2, piece)

    def tick(w, s):
        for way in (1, -1):
            if s <= reach[w, way]:
                await_bytes(slot(w, y, ring(z - s * way, 16)), zr.at[w, (1 - way) // 2, s - 1])
                spread(w, -s * way)

    def relay(w, s, action):
        for way in (1, -1):
            if s == 0 and way == 1:
                action(w, 0)
            if s > 0 and s <= reach[w, way]:
                action(w, -s * way)

    spread(0, 0)
    spread(1, 0)

    for j in range(3):
        own_b[:, 128 * j : 128 * j + 128] = jnp.broadcast_to(b_in_ref[j : j + 1, :], (8, 128))

    def step(s):
        for w, at in ((0, s), (1, s - LAG)):
            if w == 1 and at == 0:
                spread(1, 0)
            if 1 <= at <= 8:
                tick(w, at)
            if 1 <= at <= 9:
                relay(w, at - 1, pass_on)
            if 2 <= at <= 10:
                relay(w, at - 2, last)

    lane = lax.broadcasted_iota(jnp.int32, (1, 128), 1)
    columns[...] = table_ref[...].T

    def spread_table(i, carry):
        at = pl.ds(pl.multiple_of(i * 8, 8), 8)
        table = columns[at, :]
        for j in range(TAPS):
            d = j % 7 - 3
            value = jnp.broadcast_to(table[:, j : j + 1], (8, 128))
            if d != 0:
                inside = lane >= d if d > 0 else lane < 128 + d
                value = jnp.where(inside, value, 0.0)
            planes[j, at, :] = value
        diagonal = (
            lax.broadcasted_iota(jnp.int32, (8, SLAB), 0) + i * 8
            == lax.broadcasted_iota(jnp.int32, (8, SLAB), 1)
        )
        for j, ref in ((BIAS, dw_bias_ref), (OUT_BIAS, b_out_ref), (SCALE, gamma_ref)):
            column = jnp.sum(jnp.where(diagonal, ref[...], 0.0), axis=1, keepdims=True)
            planes[j, at, :] = jnp.broadcast_to(column, (8, 128))
        return carry

    lax.fori_loop(0, 12, spread_table, 0)

    def widen(i, carry):
        at = pl.ds(pl.multiple_of(i * 16, 16), 16)
        wide[:, at, :] = f_ref[:, at, :].astype(F32)
        return carry

    lax.fori_loop(0, 6, widen, 0)

    def taps(rows, at, pairs):
        total = [None] * len(pairs)
        for tap_col in range(7):
            d = tap_col - 3
            weight = {}
            for r, pair in enumerate(pairs):
                part = None
                for e, tap_row in pair:
                    if tap_row not in weight:
                        weight[tap_row] = planes[tap_row * 7 + tap_col, at, :]
                    product = rows[e] * weight[tap_row]
                    part = product if part is None else part + product
                if d != 0:
                    part = pltpu.roll(part, (-d) % 128, 1)
                total[r] = part if total[r] is None else total[r] + part
        return total

    def own_rows(i, carry):
        at = pl.ds(pl.multiple_of(i * 8, 8), 8)
        rows = [wide[r, at, :] for r in range(8)]
        pairs = [[(e, e - r + 3) for e in range(8) if 0 <= e - r + 3 < 7] for r in range(8)]
        bias = planes[BIAS, at, :]
        for r, part in enumerate(taps(rows, at, pairs)):
            conv[r, at, :] = part + bias
        return carry

    lax.fori_loop(0, 12, own_rows, 0)
    step(1)

    await_bytes(halo.at[0], halo_r.at[0])
    await_bytes(halo.at[1], halo_r.at[1])

    @pl.when(t == 0)
    def _():
        halo[0] = jnp.zeros((3, SLAB, 128), BF16)

    @pl.when(t == 31)
    def _():
        halo[1] = jnp.zeros((3, SLAB, 128), BF16)

    def rims(i, carry):
        at = pl.ds(pl.multiple_of(i * 16, 16), 16)
        for side, first in ((0, 0), (1, 5)):
            rows = [halo[side, r, at, :].astype(F32) for r in range(3)]
            if side == 0:
                pairs = [[(e, e - r) for e in range(r, 3)] for r in range(3)]
            else:
                pairs = [[(e, e - r + 6) for e in range(r + 1)] for r in range(3)]
            for r, part in enumerate(taps(rows, at, pairs)):
                cv[first + r, at, :] = (conv[first + r, at, :] + part).astype(BF16)
        for r in (3, 4):
            cv[r, at, :] = conv[r, at, :].astype(BF16)
        return carry

    lax.fori_loop(0, 6, rims, 0)

    def block(kk):
        return xg.at[:, pl.ds(pl.multiple_of(kk * SLAB, SLAB), SLAB), :]

    for r in (1, 2, 0, 3):
        rows = pl.ds(2 * ring(zh + r, 4), 2)
        send(cv.at[rows], block(k), za_s.at[r], za_r.at[r], z_at(2 + 4 * r - 16 * (r // 2)))
    for r in range(4):
        to = z_at(2 + 4 * r - 16 * (r // 2))
        send(own_b, bb.at[zh], b_s.at[r], b_r.at[r], to)

    unit = ring(z - 2, 16)
    place, line = lax.div(unit, 4), lax.rem(unit, 4)

    def source(r):
        return ring(place - r, 4)

    def share(r):
        kk = x * 4 + source(r)
        for e in (2, 1, 3):
            send(block(kk), block(kk), xa_s.at[e - 1, r], xa_r.at[e - 1, r], x_at(e))

    def arrived(r):
        await_bytes(block(x * 4 + source(r)), za_r.at[r])
        share(r)

    for s in range(2, 11):
        step(s)
        if s == FIRST:
            arrived(0)
            arrived(3)
        if s == SECOND:
            arrived(1)
            arrived(2)
    for r in range(4):
        for e in (1, 2, 3):
            await_bytes(block(ring(x - e, 4) * 4 + source(r)), xa_r.at[e - 1, r])

    def load(j):
        return xg[:, pl.ds(pl.multiple_of(j * SLAB, SLAB), SLAB), :].astype(F32)

    def fold(v):
        return jnp.sum(v.reshape(2, SLAB // 8, 8, 128), axis=1)

    zero = jnp.zeros((2, 8, 128), F32)
    total = lax.fori_loop(0, 16, lambda j, s: s + fold(load(j)), zero)
    mean = jnp.sum(total, axis=1, keepdims=True) / 1536.0

    def squares(j, s):
        centered = load(j) - mean
        return s + fold(centered * centered)

    total = lax.fori_loop(0, 16, squares, zero)
    scale = lax.rsqrt(jnp.sum(total, axis=1, keepdims=True) / 1536.0 + 1e-6)

    def normalize(j, carry):
        at = pl.ds(pl.multiple_of(j * 128, 128), 128)
        for r in range(2):
            v = (xg[r, at, :].astype(F32) - mean[r]) * scale[r]
            v = v.T * gain_ref[pl.ds(j, 1), :] + shift_ref[pl.ds(j, 1), :]
            xt[r * 128 : r * 128 + 128, at] = v.astype(BF16)
        return carry

    lax.fori_loop(0, 12, normalize, 0)

    def row(w, yy, cc):
        return W.at[w, :, pl.ds(yy * 4, 4), cc]

    def crossed(w, o):
        await_bytes(row(w, ring(y + o, 4), 1 - c), cr.at[w, o % 4])

    for r in range(4):
        await_bytes(bb.at[source(r)], b_r.at[r])
    for o in (0, -1, 1, 2):
        crossed(0, o)

    for g in range(4):
        pre = jnp.dot(xt[...], W[0, g].reshape(1536, COLS), preferred_element_type=F32)
        hid[g] = gelu(pre + bb[g, 0:1, :]).T.astype(BF16)
        if g + 11 <= LAG + 10:
            step(g + 11)

    def project(o):
        crossed(1, o)
        to_x = ring(y + o, 4)
        for half in range(2):
            part = jnp.zeros((COLS // 2, 256), F32)
            for g in range(4):
                weights = W[1, g, pl.ds(to_x * 4 + 2 * half, 2)].reshape(COLS // 2, COLS)
                part = part + jnp.dot(weights, hid[g], preferred_element_type=F32)
            part = part.astype(BF16)
            at = slice(half * (COLS // 2), (half + 1) * (COLS // 2))
            ob[to_x, 0, at] = part[:, 0:128]
            ob[to_x, 1, at] = part[:, 128:256]

        give(to_x, 0)

    def give(to_x, r):
        @pl.when(to_x != x)
        def _():
            send(
                ob.at[to_x, r], rb.at[x, r], rs_s.at[to_x, r], rs_r.at[x, r],
                device(to_x, y, z, c),
            )

    for o in (0, 1, -1, 2):
        project(o)
    for o in (0, 1, -1, 2):
        give(ring(y + o, 4), 1)

    for r in range(2):
        for e in (1, 2, 3):
            await_bytes(rb.at[ring(x + e, 4), r], rs_r.at[ring(x + e, 4), r])

        def reduce(i, carry):
            at = pl.ds(pl.multiple_of(i * 32, 32), 32)
            s = ob[x, r, at, :].astype(F32)
            for e in (1, 2, 3):
                s = s + rb[ring(x + e, 4), r, at, :].astype(F32)
            pz[r, at, :] = s.astype(BF16)
            return carry

        lax.fori_loop(0, 12, reduce, 0)
        for n in (1, 2, 0, 3):
            home = source(n)
            src = pz.at[r, pl.ds(pl.multiple_of(home * SLAB, SLAB), SLAB), :]
            send(
                src, fin.at[2 * place + r], fin_s.at[n, r], fin_r.at[n, r],
                device(x, y, home * 4 + line, c),
            )
    for r in range(2):
        for n in (0, 3, 1, 2):
            await_bytes(fin.at[2 * ring(zh + n, 4) + r], fin_r.at[n, r])

    def finish(i, carry):
        at = pl.ds(pl.multiple_of(i * 16, 16), 16)
        projected = fin[:, at, :].astype(F32) + planes[OUT_BIAS, at, :]
        o_ref[:, at, :] = (wide[:, at, :] + planes[SCALE, at, :] * projected).astype(BF16)
        return carry

    lax.fori_loop(0, 6, finish, 0)

    await_bytes(f_ref.at[5:8], halo_s.at[0])
    await_bytes(f_ref.at[0:3], halo_s.at[1])
    for n in range(4):
        await_bytes(cv.at[0:2], za_s.at[n])
        await_bytes(own_b, b_s.at[n])
        for e in range(3):
            await_bytes(cv.at[0:2], xa_s.at[e, n])
        for r in range(2):
            await_bytes(cv.at[0], fin_s.at[n, r])
            if n > 0:
                await_bytes(ob.at[0, 0], rs_s.at[ring(x + n, 4), r])
    for w in (0, 1):
        for way in (1, -1):
            count = reach[w, way]
            view = W.at[w, 0, 0:count, c]
            await_bytes(view, zs.at[w, (1 - way) // 2])
        for i in range(3):
            await_bytes(row(w, y, c), ys.at[w, i])
        for o in range(4):
            await_bytes(row(w, y, c), cs.at[w, o])


def local(features, dw_weight, dw_bias, ln_gain, ln_bias, w_in, b_in, w_out, b_out, gamma):
    dma = pltpu.SemaphoreType.DMA
    vmem = pl.BlockSpec(memory_space=pltpu.VMEM)
    return pl.pallas_call(
        body,
        out_shape=jax.ShapeDtypeStruct(features.shape, BF16),
        in_specs=[pl.BlockSpec(memory_space=pltpu.HBM)] * 10,
        out_specs=vmem,
        scratch_shapes=[
            pltpu.VMEM((8, SLAB, 128), BF16),
            pltpu.VMEM((TAPS, SLAB), F32),
            pltpu.VMEM((1, SLAB), F32),
            pltpu.VMEM((1, SLAB), F32),
            pltpu.VMEM((1, SLAB), F32),
            pltpu.VMEM((12, 128), F32),
            pltpu.VMEM((12, 128), F32),
            pltpu.VMEM((3, 128), F32),
            dma((10,)),
            pltpu.VMEM((SLAB, TAPS), F32),
            pltpu.VMEM((TAPS + 3, SLAB, 128), F32),
            pltpu.VMEM((8, SLAB, 128), F32),
            pltpu.VMEM((2, 3, SLAB, 128), BF16),
            pltpu.VMEM((8, SLAB, 128), F32),
            pltpu.VMEM((8, SLAB, 128), BF16),
            pltpu.VMEM((2, 1536, 128), BF16),
            pltpu.VMEM((256, 1536), BF16),
            pltpu.VMEM((4, COLS, 256), BF16),
            pltpu.VMEM((4, 2, COLS, 128), BF16),
            pltpu.VMEM((4, 2, COLS, 128), BF16),
            pltpu.VMEM((2, COLS, 128), BF16),
            pltpu.VMEM((8, SLAB, 128), BF16),
            pltpu.VMEM((2, 4, 16, 2, TALL, COLS), BF16),
            pltpu.VMEM((8, COLS), F32),
            pltpu.VMEM((4, 8, COLS), F32),
            dma((2,)), dma((2,)),
            dma((4,)), dma((4,)),
            dma((4,)), dma((4,)),
            dma((3, 4)), dma((3, 4)),
            dma((4, 2)), dma((4, 2)),
            dma((4, 2)), dma((4, 2)),
            dma((2, 2)), dma((2, 2, 8)),
            dma((2, 3)), dma((2, 16)), dma((2, 16)), dma((2, 16)),
            dma((2, 4)), dma((2, 4)),
        ],
        compiler_params=pltpu.CompilerParams(
            collective_id=0, has_side_effects=True, vmem_limit_bytes=62 * 2**20
        ),
        name="block",
    )(
        features, dw_weight.T, dw_bias[None, :], b_out[None, :], gamma[None, :],
        ln_gain.reshape(12, 128), ln_bias.reshape(12, 128), w_in, b_in.reshape(3, 128), w_out.T,
    )


def solution(mesh):
    placed = (
        P("tile", "chan", None),
        P("chan", None),
        P("chan"),
        P(),
        P(),
        P("tile", "chan"),
        P("chan"),
        P("chan", "tile"),
        P("chan"),
        P("chan"),
    )
    return jax.shard_map(
        local, mesh=mesh, in_specs=placed, out_specs=P("tile", "chan", None), check_vma=False
    )
```

time: 115 us -> 93.7 us (0.81)
  the two profiles are of different devices: /device:TPU:17 before, /device:TPU:8 now
where the time goes in v2:
time: 93.7 us; the launch traced here: 93.6 us
  Pallas kernels  91.9 us (98%)
  local copies, waits for them, and re-layouts  1.62 us (2%)
    pallas_call x1, Pallas kernels, local(): pl.pallas_call(body, out_shape=jax.ShapeDtypeStruct(features.shape, BF16)...  91.9 us

profile of v2, /device:TPU:8, one launch (start us, length us, event | category | flops | bytes accessed | tf_op | source)
XLA Modules:
  0.0 93.6 jit_solution(12546019099216569553)
XLA Ops:
  0.0 91.9 %block.1 = bf16[8,96,128]{2,1,0:T(8,128)(2,1)} custom-call(bf16[8,96,128]{2,1,0:T(8,128)(2,1)} %f_hbm.1, f32[49,96]{1,0:T(8,128)} %bitcast.9, f32[1,96]{1,0:T(1,128)} %bitcast.13, f32[1,96]{1,0:T(1,128)} %bitcast.14, f32[1,96]{1,0:T(1,128)} %bitcast.15, f32[12,128]{1,0:T(8,128)} %bitcast.10, f32[12,128]{1,0:T(8,128)} %bitcast.11, bf16[48,384]{1,0:T(8,128)(2,1)} %w_in_hbm.1, ...), custom_call_target="tpu_custom_call" | custom-call | tf_op jit(solution)/shard_map/block/pallas_call | solution.py:447
  92.0 1.6 %copy.12 = bf16[8,96,128]{2,1,0:T(8,128)(2,1)} copy(bf16[8,96,128]{2,1,0:T(8,128)(2,1)} %block.1) | data formatting | bytes 393216

commit v3 on v2

--- a/solution.py
+++ b/solution.py
@@ -14,9 +14,9 @@
 SLAB = 96
 COLS = 384
 TALL = 48
+HEAD = 80
 TAPS = 49
-FIRST, SECOND = 4, 6
-LAG = 0
+FIRST, SECOND = 7, 9
 BIAS, OUT_BIAS, SCALE = 49, 50, 51
 
 ERF_NUM = (
@@ -57,7 +57,7 @@
     f_ref, table_ref, dw_bias_ref, b_out_ref, gamma_ref, gain_ref, shift_ref, b_in_ref,
     fetch_s, columns, planes, wide, halo, conv, cv, xg, xt, hid, ob, rb, pz, fin, W, own_b, bb,
     halo_s, halo_r, za_s, za_r, b_s, b_r, xa_s, xa_r, rs_s, rs_r, fin_s, fin_r,
-    zs, zr, ys, yf, yb, yq, cs, cr,
+    zs, zr, ys, yf, yb, yq, cs, cr, ty_s, ty_r, ts, tr, tc_s, tc_r,
 ):
     t = lax.axis_index("tile")
     k = lax.axis_index("chan")
@@ -97,11 +97,10 @@
     def await_bytes(view, sem):
         pltpu.make_async_copy(view, view, sem).wait()
 
-    mine = y * 4 + zl
     fetches = [
         pltpu.make_async_copy(src, dst, fetch_s.at[i])
         for i, (src, dst) in enumerate((
-            (w_in_hbm, W.at[0, zh, mine, c]), (w_out_hbm, W.at[1, zh, mine, c]), (f_hbm, f_ref),
+            (w_in_hbm, W.at[zh, y, zl, c, 0:TALL]), (w_out_hbm, W.at[zh, y, zl, c, TALL : 2 * TALL]), (f_hbm, f_ref),
             (table_hbm, table_ref), (dw_bias_hbm, dw_bias_ref), (b_out_hbm, b_out_ref),
             (gamma_hbm, gamma_ref), (gain_hbm, gain_ref), (shift_hbm, shift_ref),
             (b_in_hbm, b_in_ref),
@@ -109,15 +108,21 @@
     ]
 
     barrier = pltpu.get_barrier_semaphore()
-    partners = [tile_at(1), tile_at(-1), x_at(1), x_at(2), x_at(3), y_at(1), y_at(-1)]
+    partners = [tile_at(1), tile_at(-1), x_at(1), x_at(2), x_at(3), y_at(1), y_at(2), y_at(-1)]
     partners += [z_at(1), z_at(-1), z_at(2), z_at(-2), z_at(6), z_at(-6), other]
     for partner in partners:
         pl.semaphore_signal(barrier, inc=1, device_id=partner, device_id_type=MESH)
     for fetch in fetches:
         fetch.start()
 
-    def slot(w, yy, zz):
-        return W.at[w, lax.div(zz, 4), yy * 4 + lax.rem(zz, 4), c]
+    def slot(yy, zz):
+        return W.at[lax.div(zz, 4), yy, lax.rem(zz, 4), c, 0:HEAD]
+
+    def bundle(zz):
+        return W.at[lax.div(zz, 4), :, lax.rem(zz, 4), c, HEAD : 2 * TALL]
+
+    def rest(yy):
+        return W.at[zh, yy, zl, c, HEAD : 2 * TALL]
 
     for fetch in fetches:
         fetch.wait()
@@ -126,70 +131,87 @@
     send(f_ref.at[5:8], halo.at[0], halo_s.at[0], halo_r.at[0], tile_at(1))
     send(f_ref.at[0:3], halo.at[1], halo_s.at[1], halo_r.at[1], tile_at(-1))
 
-    reach = {(0, 1): 8, (0, -1): 7, (1, 1): 7, (1, -1): 8}
-
-    def spread(w, off):
-        zz = ring(z + off, 16)
-        piece = slot(w, y, zz)
+    reach = {1: 8, -1: 7}
+
+    def along(off):
+        return [way for way in (1, -1) if off * way <= 0 and -off * way < reach[way]]
+
+    def heading(off):
+        return 1 if off <= 0 else -1
+
+    def cross(o, piece):
+        send(piece, piece, cs.at[o], cr.at[o], other)
+
+    def spread(off):
+        piece = slot(y, ring(z + off, 16))
+        for way in along(off):
+            i = (1 - way) // 2
+            send(piece, piece, zs.at[i, -off * way], zr.at[i, -off * way], z_at(way))
+        onward = heading(off)
+        send(piece, piece, ys.at[0], yf.at[off % 16], y_at(onward))
+        send(piece, piece, ys.at[1], yb.at[off % 16], y_at(-onward))
+        cross(0, piece)
+
+    def pass_on(off):
+        onward = heading(off)
+        piece = slot(ring(y - onward, 4), ring(z + off, 16))
+        await_bytes(piece, yf.at[off % 16])
+        send(piece, piece, ys.at[2], yq.at[off % 16], y_at(onward))
+        cross(-onward % 4, piece)
+        piece = slot(ring(y + onward, 4), ring(z + off, 16))
+        await_bytes(piece, yb.at[off % 16])
+        cross(onward % 4, piece)
+
+    def last(off):
+        piece = slot(ring(y + 2, 4), ring(z + off, 16))
+        await_bytes(piece, yq.at[off % 16])
+        cross(2, piece)
+
+    def tick(s):
         for way in (1, -1):
-            if off * way <= 0 and -off * way < reach[w, way]:
-                send(piece, piece, zs.at[w, (1 - way) // 2],
-                     zr.at[w, (1 - way) // 2, -off * way], z_at(way))
-        onward = heading(w, off)
-        send(piece, piece, ys.at[w, 0], yf.at[w, off % 16], y_at(onward))
-        send(piece, piece, ys.at[w, 1], yb.at[w, off % 16], y_at(-onward))
-        cross(w, 0, piece)
-
-    def cross(w, o, piece):
-        send(piece, piece, cs.at[w, o], cr.at[w, o], other)
-
-    def heading(w, off):
-        return 1 if off < 0 or (off == 0 and w == 0) else -1
-
-    def pass_on(w, off):
-        onward = heading(w, off)
-        piece = slot(w, ring(y - onward, 4), ring(z + off, 16))
-        await_bytes(piece, yf.at[w, off % 16])
-        send(piece, piece, ys.at[w, 2], yq.at[w, off % 16], y_at(onward))
-        cross(w, -onward % 4, piece)
-        piece = slot(w, ring(y + onward, 4), ring(z + off, 16))
-        await_bytes(piece, yb.at[w, off % 16])
-        cross(w, onward % 4, piece)
-
-    def last(w, off):
-        piece = slot(w, ring(y + 2, 4), ring(z + off, 16))
-        await_bytes(piece, yq.at[w, off % 16])
-        cross(w, 2, piece)
-
-    def tick(w, s):
-        for way in (1, -1):
-            if s <= reach[w, way]:
-                await_bytes(slot(w, y, ring(z - s * way, 16)), zr.at[w, (1 - way) // 2, s - 1])
-                spread(w, -s * way)
-
-    def relay(w, s, action):
+            if s <= reach[way]:
+                await_bytes(slot(y, ring(z - s * way, 16)), zr.at[(1 - way) // 2, s - 1])
+                spread(-s * way)
+
+    def relay(s, action):
         for way in (1, -1):
             if s == 0 and way == 1:
-                action(w, 0)
-            if s > 0 and s <= reach[w, way]:
-                action(w, -s * way)
-
-    spread(0, 0)
-    spread(1, 0)
+                action(0)
+            if s > 0 and s <= reach[way]:
+                action(-s * way)
+
+    def pass_bundle(off):
+        piece = bundle(ring(z + off, 16))
+        for way in along(off):
+            i = (1 - way) // 2
+            send(piece, piece, ts.at[i], tr.at[i, -off * way], z_at(way))
+        send(piece, piece, tc_s, tc_r, other)
+
+    def tick_bundle(s):
+        if s == 0:
+            for e in (1, 2, 3):
+                await_bytes(rest(ring(y - e, 4)), ty_r.at[e - 1])
+            pass_bundle(0)
+        for way in (1, -1):
+            if 0 < s <= reach[way]:
+                await_bytes(bundle(ring(z - s * way, 16)), tr.at[(1 - way) // 2, s - 1])
+                pass_bundle(-s * way)
+
+    spread(0)
+    for e in (1, 3, 2):
+        send(rest(y), rest(y), ty_s.at[e - 1], ty_r.at[e - 1], y_at(e))
 
     for j in range(3):
         own_b[:, 128 * j : 128 * j + 128] = jnp.broadcast_to(b_in_ref[j : j + 1, :], (8, 128))
 
     def step(s):
-        for w, at in ((0, s), (1, s - LAG)):
-            if w == 1 and at == 0:
-                spread(1, 0)
-            if 1 <= at <= 8:
-                tick(w, at)
-            if 1 <= at <= 9:
-                relay(w, at - 1, pass_on)
-            if 2 <= at <= 10:
-                relay(w, at - 2, last)
+        if s <= 8:
+            tick(s)
+        if s <= 9:
+            tick_bundle(s - 1)
+            relay(s - 1, pass_on)
+        if s >= 2:
+            relay(s - 2, last)
 
     lane = lax.broadcasted_iota(jnp.int32, (1, 128), 1)
     columns[...] = table_ref[...].T
@@ -342,74 +364,74 @@
 
     lax.fori_loop(0, 12, normalize, 0)
 
-    def row(w, yy, cc):
-        return W.at[w, :, pl.ds(yy * 4, 4), cc]
-
-    def crossed(w, o):
-        await_bytes(row(w, ring(y + o, 4), 1 - c), cr.at[w, o % 4])
-
+    def row(yy, cc):
+        return W.at[:, yy, :, cc, 0:HEAD]
+
+    for o in range(4):
+        await_bytes(row(ring(y + o, 4), 1 - c), cr.at[o])
+    await_bytes(W.at[:, :, :, 1 - c, HEAD : 2 * TALL], tc_r)
     for r in range(4):
         await_bytes(bb.at[source(r)], b_r.at[r])
-    for o in (0, -1, 1, 2):
-        crossed(0, o)
-
-    for g in range(4):
-        pre = jnp.dot(xt[...], W[0, g].reshape(1536, COLS), preferred_element_type=F32)
+
+    def expand(g, carry):
+        pre = jnp.dot(
+            xt[...], W[g, :, :, :, 0:TALL].reshape(1536, COLS), preferred_element_type=F32
+        )
         hid[g] = gelu(pre + bb[g, 0:1, :]).T.astype(BF16)
-        if g + 11 <= LAG + 10:
-            step(g + 11)
-
-    def project(o):
-        crossed(1, o)
+        return carry
+
+    lax.fori_loop(0, 4, expand, 0)
+
+    order = ((1, 2), (0, 3))
+
+    def project(h, o):
         to_x = ring(y + o, 4)
-        for half in range(2):
-            part = jnp.zeros((COLS // 2, 256), F32)
-            for g in range(4):
-                weights = W[1, g, pl.ds(to_x * 4 + 2 * half, 2)].reshape(COLS // 2, COLS)
-                part = part + jnp.dot(weights, hid[g], preferred_element_type=F32)
-            part = part.astype(BF16)
-            at = slice(half * (COLS // 2), (half + 1) * (COLS // 2))
-            ob[to_x, 0, at] = part[:, 0:128]
-            ob[to_x, 1, at] = part[:, 128:256]
-
-        give(to_x, 0)
-
-    def give(to_x, r):
+        part = jnp.zeros((2 * SLAB, 256), F32)
+        for g in range(4):
+            weights = jnp.concatenate(
+                [
+                    W[g, to_x, source(n), :, TALL : 2 * TALL].reshape(SLAB, COLS)
+                    for n in order[h]
+                ],
+                axis=0,
+            )
+            part = part + jnp.dot(weights, hid[g], preferred_element_type=F32)
+        part = part.astype(BF16)
+        for i in range(2):
+            for r in range(2):
+                ob[to_x, h, i, r] = part[SLAB * i : SLAB * i + SLAB, 128 * r : 128 * r + 128]
+
         @pl.when(to_x != x)
         def _():
             send(
-                ob.at[to_x, r], rb.at[x, r], rs_s.at[to_x, r], rs_r.at[x, r],
+                ob.at[to_x, h], rb.at[x, h], rs_s.at[to_x, h], rs_r.at[x, h],
                 device(to_x, y, z, c),
             )
 
-    for o in (0, 1, -1, 2):
-        project(o)
-    for o in (0, 1, -1, 2):
-        give(ring(y + o, 4), 1)
-
-    for r in range(2):
+    for h in range(2):
+        for o in (0, 1, -1, 2):
+            project(h, o)
+
+    for h in range(2):
         for e in (1, 2, 3):
-            await_bytes(rb.at[ring(x + e, 4), r], rs_r.at[ring(x + e, 4), r])
-
-        def reduce(i, carry):
-            at = pl.ds(pl.multiple_of(i * 32, 32), 32)
-            s = ob[x, r, at, :].astype(F32)
-            for e in (1, 2, 3):
-                s = s + rb[ring(x + e, 4), r, at, :].astype(F32)
-            pz[r, at, :] = s.astype(BF16)
-            return carry
-
-        lax.fori_loop(0, 12, reduce, 0)
-        for n in (1, 2, 0, 3):
-            home = source(n)
-            src = pz.at[r, pl.ds(pl.multiple_of(home * SLAB, SLAB), SLAB), :]
+            await_bytes(rb.at[ring(x + e, 4), h], rs_r.at[ring(x + e, 4), h])
+        for i in range(2):
+            def reduce(j, carry):
+                at = pl.ds(pl.multiple_of(j * 32, 32), 32)
+                total = ob[x, h, i, :, at, :].astype(F32)
+                for e in (1, 2, 3):
+                    total = total + rb[ring(x + e, 4), h, i, :, at, :].astype(F32)
+                pz[h, i, :, at, :] = total.astype(BF16)
+                return carry
+
+            lax.fori_loop(0, 3, reduce, 0)
+            n = order[h][i]
             send(
-                src, fin.at[2 * place + r], fin_s.at[n, r], fin_r.at[n, r],
-                device(x, y, home * 4 + line, c),
+                pz.at[h, i], fin.at[pl.ds(2 * place, 2)], fin_s.at[n], fin_r.at[n],
+                device(x, y, source(n) * 4 + line, c),
             )
-    for r in range(2):
-        for n in (0, 3, 1, 2):
-            await_bytes(fin.at[2 * ring(zh + n, 4) + r], fin_r.at[n, r])
+    for n in (0, 3, 1, 2):
+        await_bytes(fin.at[pl.ds(2 * ring(zh + n, 4), 2)], fin_r.at[n])
 
     def finish(i, carry):
         at = pl.ds(pl.multiple_of(i * 16, 16), 16)
@@ -426,19 +448,22 @@
         await_bytes(own_b, b_s.at[n])
         for e in range(3):
             await_bytes(cv.at[0:2], xa_s.at[e, n])
-        for r in range(2):
-            await_bytes(cv.at[0], fin_s.at[n, r])
+        await_bytes(cv.at[0:2], fin_s.at[n])
+        for h in range(2):
             if n > 0:
-                await_bytes(ob.at[0, 0], rs_s.at[ring(x + n, 4), r])
-    for w in (0, 1):
-        for way in (1, -1):
-            count = reach[w, way]
-            view = W.at[w, 0, 0:count, c]
-            await_bytes(view, zs.at[w, (1 - way) // 2])
-        for i in range(3):
-            await_bytes(row(w, y, c), ys.at[w, i])
-        for o in range(4):
-            await_bytes(row(w, y, c), cs.at[w, o])
+                await_bytes(ob.at[0, 0], rs_s.at[ring(x + n, 4), h])
+    for way in (1, -1):
+        i = (1 - way) // 2
+        await_bytes(xt.at[0 : 16 * reach[way]], ts.at[i])
+        for n in range(reach[way]):
+            await_bytes(slot(y, z), zs.at[i, n])
+    for e in range(3):
+        await_bytes(rest(y), ty_s.at[e])
+    await_bytes(W.at[:, :, :, c, HEAD : 2 * TALL], tc_s)
+    for i in range(3):
+        await_bytes(row(y, c), ys.at[i])
+    for o in range(4):
+        await_bytes(row(y, c), cs.at[o])
 
 
 def local(features, dw_weight, dw_bias, ln_gain, ln_bias, w_in, b_in, w_out, b_out, gamma):
@@ -468,11 +493,11 @@
             pltpu.VMEM((2, 1536, 128), BF16),
             pltpu.VMEM((256, 1536), BF16),
             pltpu.VMEM((4, COLS, 256), BF16),
-            pltpu.VMEM((4, 2, COLS, 128), BF16),
-            pltpu.VMEM((4, 2, COLS, 128), BF16),
-            pltpu.VMEM((2, COLS, 128), BF16),
+            pltpu.VMEM((4, 2, 2, 2, SLAB, 128), BF16),
+            pltpu.VMEM((4, 2, 2, 2, SLAB, 128), BF16),
+            pltpu.VMEM((2, 2, 2, SLAB, 128), BF16),
             pltpu.VMEM((8, SLAB, 128), BF16),
-            pltpu.VMEM((2, 4, 16, 2, TALL, COLS), BF16),
+            pltpu.VMEM((4, 4, 4, 2, 2 * TALL, COLS), BF16),
             pltpu.VMEM((8, COLS), F32),
             pltpu.VMEM((4, 8, COLS), F32),
             dma((2,)), dma((2,)),
@@ -480,10 +505,11 @@
             dma((4,)), dma((4,)),
             dma((3, 4)), dma((3, 4)),
             dma((4, 2)), dma((4, 2)),
-            dma((4, 2)), dma((4, 2)),
-            dma((2, 2)), dma((2, 2, 8)),
-            dma((2, 3)), dma((2, 16)), dma((2, 16)), dma((2, 16)),
-            dma((2, 4)), dma((2, 4)),
+            dma((4,)), dma((4,)),
+            dma((2, 8)), dma((2, 8)),
+            dma((3,)), dma((16,)), dma((16,)), dma((16,)),
+            dma((4,)), dma((4,)),
+            dma((3,)), dma((3,)), dma((2,)), dma((2, 8)), dma, dma,
         ],
         compiler_params=pltpu.CompilerParams(
             collective_id=0, has_side_effects=True, vmem_limit_bytes=62 * 2**20

time: 93.7 us -> 92.3 us (0.985)
  the two profiles are of different devices: /device:TPU:8 before, /device:TPU:6 now
where the time goes in v3:
time: 92.3 us; the launch traced here: 92.2 us
  Pallas kernels  90.5 us (98%)
  local copies, waits for them, and re-layouts  1.62 us (2%)
    pallas_call x1, Pallas kernels, local(): pl.pallas_call(body, out_shape=jax.ShapeDtypeStruct(features.shape, BF16)...  90.5 us

profile of v3, /device:TPU:6, one launch (start us, length us, event | category | flops | bytes accessed | tf_op | source)
XLA Modules:
  0.0 92.2 jit_solution(769065329169822282)
XLA Ops:
  0.0 90.5 %block.1 = bf16[8,96,128]{2,1,0:T(8,128)(2,1)} custom-call(bf16[8,96,128]{2,1,0:T(8,128)(2,1)} %f_hbm.1, f32[49,96]{1,0:T(8,128)} %bitcast.9, f32[1,96]{1,0:T(1,128)} %bitcast.13, f32[1,96]{1,0:T(1,128)} %bitcast.14, f32[1,96]{1,0:T(1,128)} %bitcast.15, f32[12,128]{1,0:T(8,128)} %bitcast.10, f32[12,128]{1,0:T(8,128)} %bitcast.11, bf16[48,384]{1,0:T(8,128)(2,1)} %w_in_hbm.1, ...), custom_call_target="tpu_custom_call" | custom-call | tf_op jit(solution)/shard_map/block/pallas_call | solution.py:472
  90.5 1.6 %copy.12 = bf16[8,96,128]{2,1,0:T(8,128)(2,1)} copy(bf16[8,96,128]{2,1,0:T(8,128)(2,1)} %block.1) | data formatting | bytes 393216

commit v4 on v3

--- a/solution.py
+++ b/solution.py
@@ -208,10 +208,11 @@
         if s <= 8:
             tick(s)
         if s <= 9:
-            tick_bundle(s - 1)
             relay(s - 1, pass_on)
         if s >= 2:
             relay(s - 2, last)
+        if s <= 9:
+            tick_bundle(s - 1)
 
     lane = lax.broadcasted_iota(jnp.int32, (1, 128), 1)
     columns[...] = table_ref[...].T

time: 92.3 us -> 91.4 us (level)
  no operation moved by 1% of the time
where the time goes in v4:
time: 91.4 us; the launch traced here: 91.2 us
  Pallas kernels  89.6 us (98%)
  local copies, waits for them, and re-layouts  1.62 us (2%)
    pallas_call x1, Pallas kernels, local(): pl.pallas_call(body, out_shape=jax.ShapeDtypeStruct(features.shape, BF16)...  89.6 us

profile of v4, /device:TPU:6, one launch (start us, length us, event | category | flops | bytes accessed | tf_op | source)
XLA Modules:
  0.0 91.2 jit_solution(10821351195569706969)
XLA Ops:
  0.0 89.6 %block.1 = bf16[8,96,128]{2,1,0:T(8,128)(2,1)} custom-call(bf16[8,96,128]{2,1,0:T(8,128)(2,1)} %f_hbm.1, f32[49,96]{1,0:T(8,128)} %bitcast.9, f32[1,96]{1,0:T(1,128)} %bitcast.13, f32[1,96]{1,0:T(1,128)} %bitcast.14, f32[1,96]{1,0:T(1,128)} %bitcast.15, f32[12,128]{1,0:T(8,128)} %bitcast.10, f32[12,128]{1,0:T(8,128)} %bitcast.11, bf16[48,384]{1,0:T(8,128)(2,1)} %w_in_hbm.1, ...), custom_call_target="tpu_custom_call" | custom-call | tf_op jit(solution)/shard_map/block/pallas_call | solution.py:473
  89.6 1.6 %copy.12 = bf16[8,96,128]{2,1,0:T(8,128)(2,1)} copy(bf16[8,96,128]{2,1,0:T(8,128)(2,1)} %block.1) | data formatting | bytes 393216
